TPU v7x, 512 devices: a whole 4x4x16 slice. The times are simulated.
512 devices in a mesh: grp: 16 (over z), seq: 32 (over y, x, core).
Axes of the slice: x: 4, y: 4, z: 16, core: 2. Of those that a mesh axis runs over, the one named last changes fastest.
Arguments:
- frames: bfloat16 [131072, 1024], P(('grp', 'seq')), parts along dimension 0, may hold values from -6 to 6
- w_qkv: bfloat16 [1024, 3072], P(None, 'seq'), may hold values from -2 to 2
- w_out: bfloat16 [1024, 1024], replicated, may hold values from -0.75 to 0.75
- dw_kernel: float32 [31, 1024], replicated, may hold values from -1 to 1
- conv_gain: float32 [1024], replicated, may hold values from 0.5 to 2
- conv_bias: float32 [1024], replicated, may hold values from -3 to 3
- rec_ids: int32 [131072], P('grp'), parts along dimension 0, may hold values from 0 to 7, never falling along the last dimension, each value on 1 to 2048 neighbouring positions
- left_spans: int32 [1024], P('grp'), parts along dimension 0, may hold values from 0 to 2, as said below
Outputs:
- block_out: bfloat16 [131072, 1024], P(('grp', 'seq')), parts along dimension 0
There are 16 independent parts, one for each index of `grp`. A program takes and returns all parts, laid end to end along the dimension named above; an argument that names none is the same for every part. Nothing has to cross between parts.
Inputs may be any that keep to these rules, and one draw needn't show every extreme that they name: `left_spans`: each entry is 0 to 2; at least one span has 2 and at least one has 0.
All inputs are finite; a program needn't handle non-finite values.
Results may differ from a plain program's by a relative error of at most 0.0064.
Values may be sent and summed in bfloat16 or wider, within the bound.
A program may use at most 64 MiB of HBM per device.

v0:
```python
import jax
import jax.numpy as jnp
from jax import lax
from jax.sharding import PartitionSpec as P

HEAD = 64
KERNEL = 31
HALF = 15
SPAN = 128
LMAX = 2


def shifted_2(block, axis, distance):
    devices = range(lax.axis_size(axis))
    route = [(i - distance, i) for i in devices if i - distance in devices]
    return lax.ppermute(block, axis, route)


def extended(block, sides, width):
    for axis, dim in sides:
        count = lax.axis_size(axis)
        forward = [(i, i + 1) for i in range(count - 1)]
        backward = [(target, source) for source, target in forward]
        low = lax.ppermute(
            lax.slice_in_dim(block, block.shape[dim] - width, None, axis=dim), axis, forward
        )
        high = lax.ppermute(lax.slice_in_dim(block, 0, width, axis=dim), axis, backward)
        block = jnp.concatenate([low, block, high], axis=dim)
    return block


def layer_norm(values):
    centred = values - jnp.mean(values, axis=-1, keepdims=True)
    return centred / jnp.sqrt(jnp.mean(centred * centred, axis=-1, keepdims=True) + 1e-05)


def on_device(frames, w_qkv, w_out, dw_kernel, conv_gain, conv_bias, rec_ids, left_spans):
    rows = frames.shape[0]
    width_model = frames.shape[1]
    device = lax.axis_index("seq")
    base = device * rows
    context = LMAX * SPAN
    window = context + SPAN
    inputs = frames.astype(jnp.float32)
    normed = layer_norm(inputs).astype(jnp.bfloat16)
    full_weights = lax.all_gather(w_qkv, "seq", axis=1, tiled=True)
    projected = jnp.dot(normed, full_weights, preferred_element_type=jnp.float32).astype(
        jnp.bfloat16
    )
    queries = projected[:, :width_model]
    keys = projected[:, width_model : 2 * width_model]
    values = projected[:, 2 * width_model :]
    prev_keys, prev_values = shifted_2((keys, values), "seq", 1)
    key_all = jnp.concatenate([prev_keys, keys], axis=0)
    value_all = jnp.concatenate([prev_values, values], axis=0)
    heads_count = width_model // HEAD
    key_ext = key_all.reshape(rows + context, heads_count, HEAD)
    value_ext = value_all.reshape(rows + context, heads_count, HEAD)
    query_heads = queries.reshape(rows, heads_count, HEAD)
    rec_front = jnp.pad(rec_ids, (context, 0), constant_values=-1)
    rec_window = lax.dynamic_slice_in_dim(rec_front, base, rows + context, 0)
    per_device = rows // SPAN
    scale = 1.0 / HEAD**0.5

    def one_span(local):
        first = local * SPAN
        global_span = device * per_device + local
        q_block = lax.dynamic_slice_in_dim(query_heads, first, SPAN, 0)
        k_block = lax.dynamic_slice_in_dim(key_ext, first, window, 0)
        v_block = lax.dynamic_slice_in_dim(value_ext, first, window, 0)
        rec_key = lax.dynamic_slice_in_dim(rec_window, first, window, 0)
        rec_query = lax.dynamic_slice_in_dim(rec_window, first + context, SPAN, 0)
        key_pos = base + first - context + jnp.arange(window, dtype=jnp.int32)
        key_span = jnp.floor_divide(key_pos, SPAN)
        lowest = global_span - lax.dynamic_index_in_dim(left_spans, global_span, 0, keepdims=False)
        allowed = (
            (key_pos >= 0)[None, :]
            & (key_span >= lowest)[None, :]
            & (rec_key[None, :] == rec_query[:, None])
        )
        scores = (
            jnp.einsum("qhd,khd->hqk", q_block, k_block, preferred_element_type=jnp.float32) * scale
        )
        scores = jnp.where(allowed[None], scores, -1e30)
        top = jnp.max(scores, axis=-1, keepdims=True)
        expo = jnp.where(allowed[None], jnp.exp(scores - top), 0.0)
        weights = (expo / jnp.sum(expo, axis=-1, keepdims=True)).astype(jnp.bfloat16)
        out = jnp.einsum("hqk,khd->qhd", weights, v_block, preferred_element_type=jnp.float32)
        return out.reshape(SPAN, width_model).astype(jnp.bfloat16)

    attended = lax.map(one_span, jnp.arange(per_device, dtype=jnp.int32)).reshape(rows, width_model)
    mid = (inputs + jnp.dot(attended, w_out, preferred_element_type=jnp.float32)).astype(
        jnp.bfloat16
    )
    cnormed = layer_norm(mid.astype(jnp.float32)).astype(jnp.bfloat16)
    padded = extended(cnormed, (("seq", 0),), HALF).astype(jnp.float32)
    rec_both = jnp.pad(rec_ids, (HALF, HALF), constant_values=-1)
    rec_conv = lax.dynamic_slice_in_dim(rec_both, base, rows + 2 * HALF, 0)
    rec_own = rec_conv[HALF : HALF + rows]
    conv = jnp.zeros((rows, width_model), jnp.float32)
    for tap in range(KERNEL):
        same = (rec_conv[tap : tap + rows] == rec_own)[:, None]
        conv = conv + jnp.where(same, dw_kernel[tap][None, :] * padded[tap : tap + rows], 0.0)
    shifted = conv_gain[None, :] * conv + conv_bias[None, :]
    return (mid.astype(jnp.float32) + shifted * jax.nn.sigmoid(shifted)).astype(jnp.bfloat16)


def solution(mesh):
    in_specs = (P(("grp", "seq"), None), P(None, "seq"), P(), P(), P(), P(), P("grp"), P("grp"))
    out_specs = P(("grp", "seq"), None)
    return jax.shard_map(
        on_device, mesh=mesh, in_specs=in_specs, out_specs=out_specs, check_vma=False
    )
```

profile of v0, /device:TPU:7, one launch (start us, length us, event | category | flops | bytes accessed | tf_op | source)
XLA Modules:
  0.0 168.2 jit_solution(4063131780693369533)
XLA Ops:
  6.5 0.0 copy-start
  6.5 0.0 all-gather.2.cloned.1.call-start
  6.5 0.7 all-gather.2.cloned.1.call-update
  7.3 0.8 pad_dynamic-slice_fusion
  8.1 1.2 convert_reduce_fusion.1
  9.3 1.3 fusion.28
  10.6 0.7 slice_compare_fusion.29
  11.3 0.7 slice_compare_fusion.28
  11.9 1.1 fusion.100
  13.0 65.9 %all-gather.2.cloned.1.call-done = bf16[1024,3072]{0,1:T(8,128)(2,1)} async-done(((bf16[1024,96]{0,1:T(8,128)(2,1)}), bf16[1024,3072]{0,1:T(8,128)(2,1)}) %all-gather.2.cloned.1.call-update) | async-done | bytes 6291472 | tf_op jit(solution)/shard_map/all_gather | solution.py:46
  79.0 4.9 %convolution_convert_fusion = bf16[256,3072]{1,0:T(8,128)(2,1)S(1)} fusion(bf16[1024,3072]{0,1:T(8,128)(2,1)} %all-gather.2.cloned.1.call-done, bf16[256,1024]{1,0:T(8,128)(2,1)} %param.10, f32[256]{0:T(256)S(1)} %add_sqrt_fusion.1, f32[256]{0:T(256)S(1)} %broadcast_multiply_fusion.1), kind=kOutput, calls=%fused_computation.32 | convolution fusion | flops 1612447744 | bytes 8390656 | tf_op jit(solution)/shard_map/dot_general | solution.py:47
  83.9 0.0 copy-start.2
  83.9 0.0 copy-start.3
  83.9 0.9 fusion.97
  84.8 3.3 %collective-permute-start.1 = (bf16[256,1024]{1,0:T(8,128)(2,1)S(1)}, bf16[256,1024]{1,0:T(8,128)(2,1)}, u32[]{:S(2)}, u32[]{:S(2)}) collective-permute-start(bf16[256,1024]{1,0:T(8,128)(2,1)S(1)} %get-tuple-element.168), channel_id=1, source_target_pairs={{0,1},{1,2},{2,3},{3,4},{4,5},{5,6},{6,7},{7,8},{8,9},{9,10},{10,1... | collective-permute-start | bytes 1572872 | tf_op jit(solution)/shard_map/ppermute | solution.py:16
  88.1 2.2 %collective-permute-start = (bf16[256,1024]{1,0:T(8,128)(2,1)}, bf16[256,1024]{1,0:T(8,128)(2,1)}, u32[]{:S(2)}, u32[]{:S(2)}) collective-permute-start(bf16[256,1024]{1,0:T(8,128)(2,1)} %get-tuple-element.170), channel_id=1, source_target_pairs={{0,1},{1,2},{2,3},{3,4},{4,5},{5,6},{6,7},{7,8},{8,9},{9,10},{10,1... | collective-permute-start | bytes 1572872 | tf_op jit(solution)/shard_map/ppermute | solution.py:16
  90.3 0.7 slice_compare_fusion.27
  91.0 0.0 copy-done.2
  91.0 0.1 pad_dynamic-slice_fusion.1
  91.1 0.0 copy-done.3
  91.1 0.1 fusion.99
  91.1 1.0 copy.13
  92.1 2.1 %collective-permute-done.1 = bf16[256,1024]{1,0:T(8,128)(2,1)} collective-permute-done((bf16[256,1024]{1,0:T(8,128)(2,1)S(1)}, bf16[256,1024]{1,0:T(8,128)(2,1)}, u32[]{:S(2)}, u32[]{:S(2)}) %collective-permute-start.1) | collective-permute-done | bytes 524320 | tf_op jit(solution)/shard_map/ppermute | solution.py:16
  94.2 2.1 %pad_maximum_fusion.1 = bf16[512,1024]{1,0:T(8,128)(2,1)} fusion(bf16[256,1024]{1,0:T(8,128)(2,1)S(1)} %get-tuple-element.168, bf16[256,1024]{1,0:T(8,128)(2,1)} %collective-permute-done.1), kind=kLoop, calls=%fused_computation.143 | loop fusion | flops 2097152 | bytes 2097152 | tf_op jit(solution)/shard_map/concatenate | solution.py:54
  96.3 1.5 copy.14
  97.8 2.1 %collective-permute-done = bf16[256,1024]{1,0:T(8,128)(2,1)} collective-permute-done((bf16[256,1024]{1,0:T(8,128)(2,1)}, bf16[256,1024]{1,0:T(8,128)(2,1)}, u32[]{:S(2)}, u32[]{:S(2)}) %collective-permute-start) | collective-permute-done | bytes 524320 | tf_op jit(solution)/shard_map/ppermute | solution.py:16
  99.9 2.3 %pad_maximum_fusion = bf16[512,1024]{1,0:T(8,128)(2,1)} fusion(bf16[256,1024]{1,0:T(8,128)(2,1)} %get-tuple-element.170, bf16[256,1024]{1,0:T(8,128)(2,1)} %collective-permute-done), kind=kLoop, calls=%fused_computation.142 | loop fusion | flops 2097152 | bytes 2097152 | tf_op jit(solution)/shard_map/concatenate | solution.py:55
  102.2 2.3 %copy.12 = bf16[512,1024]{0,1:T(8,128)(2,1)} copy(bf16[512,1024]{1,0:T(8,128)(2,1)} %pad_maximum_fusion) | data formatting | bytes 2097152 | tf_op jit(solution)/shard_map/concatenate | solution.py:55
  104.5 0.6 iota.11
  105.1 32.3 %while.12 = (s32[]{:T(128)}, bf16[2,128,1024]{2,1,0:T(8,128)(2,1)}, s32[2]{0:T(128)}, bf16[512,16,64]{0,2,1:T(8,128)(2,1)}, s32[]{:T(128)}, /*index=5*/s32[]{:T(...) while((s32[]{:T(128)}, bf16[2,128,1024]{2,1,0:T(8,128)(2,1)}, ...), condition=%wide.region_5.6_spmd, body=%wide.region_2.5_spmd.sunk | while | flops 208641536 | bytes 20045488 | solution.py:91
  105.1 1.3 dynamic_slice.70
  107.1 3.2 %fusion.114 = f32[16,128,384]{2,1,0:T(8,128)} fusion(bf16[512,16,64]{0,2,1:T(8,128)(2,1)S(1)} %get-tuple-element.346, s32[]{:T(128)S(6)} %select_n.416, bf16[256,16,64]{0,2,1:T(8,128)(2,1)} %get-tuple-element.345, s32[]{:T(128)S(6)} %select_n.417), kind=kOutput, calls=%fused_computation.10.clone.1 | convolution fusion | flops 100663296 | bytes 4194312 | tf_op jit(solution)/shard_map/while/body/eval_jaxpr/qhd,khd->hqk/dot_general | solution.py:82
  111.0 1.3 dynamic_slice.73
  113.0 0.1 dynamic_slice.72
  113.1 0.1 dynamic_slice.71
  113.2 0.1 compare_and_fusion.2
  113.3 0.0 copy-start.1
  113.3 4.5 %fusion.116 = (f32[16,128]{1,0:T(8,128)S(1)}, f32[16,128,384]{2,1,0:T(8,128)S(1)}) fusion(f32[16,128,384]{2,1,0:T(8,128)} %fusion.114, pred[128,384]{1,0:T(8,128)(4,1)S(1)} %compare_and_fusion.2), kind=kOutput, calls=%fused_computation.183.clone.1 | output fusion | flops 5505407 | bytes 6348800 | tf_op jit(solution)/shard_map/while/body/eval_jaxpr/sub | solution.py:86
  117.8 0.0 copy-done.1
  117.8 1.6 fusion.117
  119.4 1.1 copy.19
  120.5 0.7 constant_dynamic-update-slice_fusion.2
  121.2 1.3 dynamic_slice.70
  123.2 3.2 %fusion.114 = f32[16,128,384]{2,1,0:T(8,128)} fusion(bf16[512,16,64]{0,2,1:T(8,128)(2,1)S(1)} %get-tuple-element.346, s32[]{:T(128)S(6)} %select_n.416, bf16[256,16,64]{0,2,1:T(8,128)(2,1)} %get-tuple-element.345, s32[]{:T(128)S(6)} %select_n.417), kind=kOutput, calls=%fused_computation.10.clone.1 | convolution fusion | flops 100663296 | bytes 4194312 | tf_op jit(solution)/shard_map/while/body/eval_jaxpr/qhd,khd->hqk/dot_general | solution.py:82
  127.1 1.3 dynamic_slice.73
  129.1 0.1 dynamic_slice.72
  129.2 0.1 dynamic_slice.71
  129.3 0.1 compare_and_fusion.2
  129.4 0.0 copy-start.1
  129.4 4.5 %fusion.116 = (f32[16,128]{1,0:T(8,128)S(1)}, f32[16,128,384]{2,1,0:T(8,128)S(1)}) fusion(f32[16,128,384]{2,1,0:T(8,128)} %fusion.114, pred[128,384]{1,0:T(8,128)(4,1)S(1)} %compare_and_fusion.2), kind=kOutput, calls=%fused_computation.183.clone.1 | output fusion | flops 5505407 | bytes 6348800 | tf_op jit(solution)/shard_map/while/body/eval_jaxpr/sub | solution.py:86
  133.9 0.0 copy-done.1
  133.9 1.6 fusion.117
  135.5 1.1 copy.19
  136.6 0.7 constant_dynamic-update-slice_fusion.2
  137.6 2.0 %convert_reduce_fusion = (f32[256]{0:T(256)S(1)}, bf16[256,1024]{1,0:T(8,128)(2,1)S(1)}) fusion(bf16[256,1024]{1,0:T(8,128)(2,1)} %bitcast.84, bf16[1024,1024]{1,0:T(8,128)(2,1)S(1)} %copy-done, bf16[256,1024]{1,0:T(8,128)(2,1)} %param.10), kind=kOutput, calls=%fused_computation.35 | convolution fusion | flops 538181376 | bytes 3671040 | tf_op jit(solution)/shard_map/dot_general | solution.py:92
  139.6 0.3 fusion.26
  139.9 0.2 fusion.27
  140.1 6.5 %collective-permute-start.2 = (bf16[15,1024]{1,0:T(8,128)(2,1)S(1)}, bf16[15,1024]{1,0:T(8,128)(2,1)S(1)}, u32[]{:S(2)}, u32[]{:S(2)}) collective-permute-start(bf16[15,1024]{1,0:T(8,128)(2,1)S(1)} %get-tuple-element.171), channel_id=1, source_target_pairs={{0,1},{1,2},{2,3},{3,4},{4,5},{5,6},{6,7},{7,8},{8,9},{9,10},{10,1... | collective-permute-start | bytes 92168 | tf_op jit(solution)/shard_map/ppermute | solution.py:24
  146.6 1.9 %collective-permute-start.3 = (bf16[15,1024]{1,0:T(8,128)(2,1)S(1)}, bf16[15,1024]{1,0:T(8,128)(2,1)S(1)}, u32[]{:S(2)}, u32[]{:S(2)}) collective-permute-start(bf16[15,1024]{1,0:T(8,128)(2,1)S(1)} %get-tuple-element.172), channel_id=1, source_target_pairs={{1,0},{2,1},{3,2},{4,3},{5,4},{6,5},{7,6},{8,7},{9,8},{10,9},{11,1... | collective-permute-start | bytes 92168 | tf_op jit(solution)/shard_map/ppermute | solution.py:27
  148.6 0.1 slice_compare_fusion.26
  148.6 0.0 collective-permute-done.2
  148.6 5.3 %collective-permute-done.3 = bf16[15,1024]{1,0:T(8,128)(2,1)S(1)} collective-permute-done((bf16[15,1024]{1,0:T(8,128)(2,1)S(1)}, bf16[15,1024]{1,0:T(8,128)(2,1)S(1)}, u32[]{:S(2)}, u32[]{:S(2)}) %collective-permute-start.3) | collective-permute-done | bytes 30752 | tf_op jit(solution)/shard_map/ppermute | solution.py:27
  154.0 0.2 maximum_convert_fusion
  154.4 7.0 %fusion.30 = bf16[256,1024]{1,0:T(8,128)(2,1)} fusion(bf16[256,1024]{1,0:T(8,128)(2,1)S(1)} %get-tuple-element.235, f32[286,1024]{1,0:T(8,128)S(1)} %maximum_convert_fusion, f32[1024]{0:T(1024)S(1)} %copy-done.4, f32[1024]{0:T(1024)S(1)} %bitcast.63, f32[1024]{0:T(1024)S(1)} %bitcast.64, f32[1024]{0:T(1024)S(1)} %bitcast.66, f32[1024]{0:T(1024)S(1)} %bitcast.67, ...), kind=kLoop, calls=%fused_computation.48 | loop fusion | flops 26214400 | bytes 33697280 | tf_op jit(solution)/shard_map/convert_element_type | solution.py:105
  (61 shorter events, 0.2 us)
Async XLA Ops:
  6.5 130.8 %copy-start = (bf16[1024,1024]{1,0:T(8,128)(2,1)S(1)}, bf16[1024,1024]{1,0:T(8,128)(2,1)}, u32[]{:S(2)}) copy-start(bf16[1024,1024]{1,0:T(8,128)(2,1)} %param.12) | copy-start | bytes 6291460
  6.5 72.4 %all-gather.2.cloned.1.call-start = ((), (), s32[]{:S(2)}) async-start(), calls=%async_computation | async-start | bytes 6488064 | tf_op jit(solution)/shard_map/all_gather | solution.py:46
  83.9 7.1 %copy-start.2 = (s32[8192]{0:T(1024)S(1)}, s32[8192]{0:T(1024)}, u32[]{:S(2)}) copy-start(s32[8192]{0:T(1024)} %param.16) | copy-start | bytes 98308
  83.9 7.2 %copy-start.3 = (f32[31,1024]{1,0:T(8,128)S(1)}, f32[31,1024]{1,0:T(8,128)}, u32[]{:S(2)}) copy-start(f32[31,1024]{1,0:T(8,128)} %param.13) | copy-start | bytes 380932
  84.8 9.4 %collective-permute-start.1 = (bf16[256,1024]{1,0:T(8,128)(2,1)S(1)}, bf16[256,1024]{1,0:T(8,128)(2,1)}, u32[]{:S(2)}, u32[]{:S(2)}) collective-permute-start(bf16[256,1024]{1,0:T(8,128)(2,1)S(1)} %get-tuple-element.168), channel_id=1, source_target_pairs={{0,1},{1,2},{2,3},{3,4},{4,5},{5,6},{6,7},{7,8},{8,9},{9,10},{10,1... | collective-permute-start | bytes 1572872 | tf_op jit(solution)/shard_map/ppermute | solution.py:16
  88.1 11.8 %collective-permute-start = (bf16[256,1024]{1,0:T(8,128)(2,1)}, bf16[256,1024]{1,0:T(8,128)(2,1)}, u32[]{:S(2)}, u32[]{:S(2)}) collective-permute-start(bf16[256,1024]{1,0:T(8,128)(2,1)} %get-tuple-element.170), channel_id=1, source_target_pairs={{0,1},{1,2},{2,3},{3,4},{4,5},{5,6},{6,7},{7,8},{8,9},{9,10},{10,1... | collective-permute-start | bytes 1572872 | tf_op jit(solution)/shard_map/ppermute | solution.py:16
  113.3 4.5 %copy-start.1 = (bf16[512,16,64]{0,2,1:T(8,128)(2,1)S(1)}, bf16[512,16,64]{0,2,1:T(8,128)(2,1)}, u32[]{:S(2)}) copy-start(bf16[512,16,64]{0,2,1:T(8,128)(2,1)} %get-tuple-element.340) | copy-start | bytes 3145732 | tf_op jit(solution)/shard_map/while
  129.4 4.5 %copy-start.1 = (bf16[512,16,64]{0,2,1:T(8,128)(2,1)S(1)}, bf16[512,16,64]{0,2,1:T(8,128)(2,1)}, u32[]{:S(2)}) copy-start(bf16[512,16,64]{0,2,1:T(8,128)(2,1)} %get-tuple-element.340) | copy-start | bytes 3145732 | tf_op jit(solution)/shard_map/while
  137.3 16.8 %copy-start.4 = (f32[1024]{0:T(1024)S(1)}, f32[1024]{0:T(1024)}, u32[]{:S(2)}) copy-start(f32[1024]{0:T(1024)} %param.15) | copy-start | bytes 12292
  137.3 16.8 %copy-start.5 = (f32[1024]{0:T(1024)S(1)}, f32[1024]{0:T(1024)}, u32[]{:S(2)}) copy-start(f32[1024]{0:T(1024)} %param.14) | copy-start | bytes 12292
  137.3 16.8 %copy-start.6 = (pred[256]{0:T(512)(128)(4,1)S(1)}, pred[256]{0:T(512)(128)(4,1)}, u32[]{:S(2)}) copy-start(pred[256]{0:T(512)(128)(4,1)} %get-tuple-element.207) | copy-start | bytes 772
  137.3 16.8 %copy-start.7 = (pred[256]{0:T(512)(128)(4,1)S(1)}, pred[256]{0:T(512)(128)(4,1)}, u32[]{:S(2)}) copy-start(pred[256]{0:T(512)(128)(4,1)} %get-tuple-element.208) | copy-start | bytes 772
  137.3 16.8 %copy-start.8 = (pred[256]{0:T(512)(128)(4,1)S(1)}, pred[256]{0:T(512)(128)(4,1)}, u32[]{:S(2)}) copy-start(pred[256]{0:T(512)(128)(4,1)} %get-tuple-element.209) | copy-start | bytes 772
  137.4 16.8 %copy-start.9 = (pred[256]{0:T(512)(128)(4,1)S(1)}, pred[256]{0:T(512)(128)(4,1)}, u32[]{:S(2)}) copy-start(pred[256]{0:T(512)(128)(4,1)} %get-tuple-element.210) | copy-start | bytes 772
  137.4 16.8 %copy-start.10 = (pred[256]{0:T(512)(128)(4,1)S(1)}, pred[256]{0:T(512)(128)(4,1)}, u32[]{:S(2)}) copy-start(pred[256]{0:T(512)(128)(4,1)} %get-tuple-element.211) | copy-start | bytes 772
  137.4 16.8 %copy-start.11 = (pred[256]{0:T(512)(128)(4,1)S(1)}, pred[256]{0:T(512)(128)(4,1)}, u32[]{:S(2)}) copy-start(pred[256]{0:T(512)(128)(4,1)} %get-tuple-element.212) | copy-start | bytes 772
  137.4 16.8 %copy-start.12 = (pred[256]{0:T(512)(128)(4,1)S(1)}, pred[256]{0:T(512)(128)(4,1)}, u32[]{:S(2)}) copy-start(pred[256]{0:T(512)(128)(4,1)} %get-tuple-element.213) | copy-start | bytes 772
  137.4 16.8 %copy-start.13 = (pred[256]{0:T(512)(128)(4,1)S(1)}, pred[256]{0:T(512)(128)(4,1)}, u32[]{:S(2)}) copy-start(pred[256]{0:T(512)(128)(4,1)} %get-tuple-element.214) | copy-start | bytes 772
  137.4 16.8 %copy-start.14 = (pred[256]{0:T(512)(128)(4,1)S(1)}, pred[256]{0:T(512)(128)(4,1)}, u32[]{:S(2)}) copy-start(pred[256]{0:T(512)(128)(4,1)} %get-tuple-element.215) | copy-start | bytes 772
  137.4 16.8 %copy-start.15 = (pred[256]{0:T(512)(128)(4,1)S(1)}, pred[256]{0:T(512)(128)(4,1)}, u32[]{:S(2)}) copy-start(pred[256]{0:T(512)(128)(4,1)} %get-tuple-element.216) | copy-start | bytes 772
  137.4 16.8 %copy-start.16 = (pred[256]{0:T(512)(128)(4,1)S(1)}, pred[256]{0:T(512)(128)(4,1)}, u32[]{:S(2)}) copy-start(pred[256]{0:T(512)(128)(4,1)} %get-tuple-element.217) | copy-start | bytes 772
  137.4 16.8 %copy-start.17 = (pred[256]{0:T(512)(128)(4,1)S(1)}, pred[256]{0:T(512)(128)(4,1)}, u32[]{:S(2)}) copy-start(pred[256]{0:T(512)(128)(4,1)} %get-tuple-element.218) | copy-start | bytes 772
  137.4 16.8 %copy-start.18 = (pred[256]{0:T(512)(128)(4,1)S(1)}, pred[256]{0:T(512)(128)(4,1)}, u32[]{:S(2)}) copy-start(pred[256]{0:T(512)(128)(4,1)} %get-tuple-element.219) | copy-start | bytes 772
  137.5 16.8 %copy-start.19 = (pred[256]{0:T(512)(128)(4,1)S(1)}, pred[256]{0:T(512)(128)(4,1)}, u32[]{:S(2)}) copy-start(pred[256]{0:T(512)(128)(4,1)} %get-tuple-element.220) | copy-start | bytes 772
  137.5 16.8 %copy-start.20 = (pred[256]{0:T(512)(128)(4,1)S(1)}, pred[256]{0:T(512)(128)(4,1)}, u32[]{:S(2)}) copy-start(pred[256]{0:T(512)(128)(4,1)} %get-tuple-element.221) | copy-start | bytes 772
  137.5 16.8 %copy-start.21 = (pred[256]{0:T(512)(128)(4,1)S(1)}, pred[256]{0:T(512)(128)(4,1)}, u32[]{:S(2)}) copy-start(pred[256]{0:T(512)(128)(4,1)} %get-tuple-element.222) | copy-start | bytes 772
  137.5 16.8 %copy-start.22 = (pred[256]{0:T(512)(128)(4,1)S(1)}, pred[256]{0:T(512)(128)(4,1)}, u32[]{:S(2)}) copy-start(pred[256]{0:T(512)(128)(4,1)} %get-tuple-element.223) | copy-start | bytes 772
  137.5 16.8 %copy-start.23 = (pred[256]{0:T(512)(128)(4,1)S(1)}, pred[256]{0:T(512)(128)(4,1)}, u32[]{:S(2)}) copy-start(pred[256]{0:T(512)(128)(4,1)} %get-tuple-element.224) | copy-start | bytes 772
  137.5 16.8 %copy-start.24 = (pred[256]{0:T(512)(128)(4,1)S(1)}, pred[256]{0:T(512)(128)(4,1)}, u32[]{:S(2)}) copy-start(pred[256]{0:T(512)(128)(4,1)} %get-tuple-element.225) | copy-start | bytes 772
  137.5 16.8 %copy-start.25 = (pred[256]{0:T(512)(128)(4,1)S(1)}, pred[256]{0:T(512)(128)(4,1)}, u32[]{:S(2)}) copy-start(pred[256]{0:T(512)(128)(4,1)} %get-tuple-element.226) | copy-start | bytes 772
  137.5 16.8 %copy-start.26 = (pred[256]{0:T(512)(128)(4,1)S(1)}, pred[256]{0:T(512)(128)(4,1)}, u32[]{:S(2)}) copy-start(pred[256]{0:T(512)(128)(4,1)} %get-tuple-element.227) | copy-start | bytes 772
  137.5 16.8 %copy-start.27 = (pred[256]{0:T(512)(128)(4,1)S(1)}, pred[256]{0:T(512)(128)(4,1)}, u32[]{:S(2)}) copy-start(pred[256]{0:T(512)(128)(4,1)} %get-tuple-element.228) | copy-start | bytes 772
  137.5 16.8 %copy-start.28 = (pred[256]{0:T(512)(128)(4,1)S(1)}, pred[256]{0:T(512)(128)(4,1)}, u32[]{:S(2)}) copy-start(pred[256]{0:T(512)(128)(4,1)} %get-tuple-element.229) | copy-start | bytes 772
  137.6 16.8 %copy-start.29 = (pred[256]{0:T(512)(128)(4,1)S(1)}, pred[256]{0:T(512)(128)(4,1)}, u32[]{:S(2)}) copy-start(pred[256]{0:T(512)(128)(4,1)} %get-tuple-element.230) | copy-start | bytes 772
  140.1 8.5 %collective-permute-start.2 = (bf16[15,1024]{1,0:T(8,128)(2,1)S(1)}, bf16[15,1024]{1,0:T(8,128)(2,1)S(1)}, u32[]{:S(2)}, u32[]{:S(2)}) collective-permute-start(bf16[15,1024]{1,0:T(8,128)(2,1)S(1)} %get-tuple-element.171), channel_id=1, source_target_pairs={{0,1},{1,2},{2,3},{3,4},{4,5},{5,6},{6,7},{7,8},{8,9},{9,10},{10,1... | collective-permute-start | bytes 92168 | tf_op jit(solution)/shard_map/ppermute | solution.py:24
  146.6 7.3 %collective-permute-start.3 = (bf16[15,1024]{1,0:T(8,128)(2,1)S(1)}, bf16[15,1024]{1,0:T(8,128)(2,1)S(1)}, u32[]{:S(2)}, u32[]{:S(2)}) collective-permute-start(bf16[15,1024]{1,0:T(8,128)(2,1)S(1)} %get-tuple-element.172), channel_id=1, source_target_pairs={{1,0},{2,1},{3,2},{4,3},{5,4},{6,5},{7,6},{8,7},{9,8},{10,9},{11,1... | collective-permute-start | bytes 92168 | tf_op jit(solution)/shard_map/ppermute | solution.py:27
Sparse Core Ops, SparseCore 0:
  10.5 68.4 all-gather.1
where the time goes:
time: 169 us; the launch traced here: 168 us
  waiting for transfers between devices  76.2 us (45%)
  other arithmetic  25.9 us (15%)
  local copies, waits for them, and re-layouts  17.7 us (10%)
  matrix products  16.5 us (10%)
  starting transfers between devices  13.9 us (8%)
  between operations  13.9 us (8%)
  loops' own time  4.22 us (2%)
    all_gather x1, waiting for transfers between devices, on_device(): full_weights = lax.all_gather(w_qkv, 'seq', axis=1, tiled=True)  65.9 us
    sub x2, other arithmetic, one_span(): expo = jnp.where(allowed[None], jnp.exp(scores - top), 0.0)  8.96 us
    convert_element_type x1, other arithmetic, on_device(): (mid.astype(jnp.float32) + shifted * jax.nn.sigmoid(shifted)).astype(jnp....  7 us
    ppermute x1, starting transfers between devices, extended(): lax.ppermute(lax.slice_in_dim(block, block.shape[dim] - width, None, axis...  6.5 us
    dot_general x2, matrix products, one_span(): jnp.einsum('qhd,khd->hqk', q_block, k_block, preferred_element_type=jnp.f...  6.41 us
    ppermute x2, starting transfers between devices, shifted_2(): return lax.ppermute(block, axis, route)  5.44 us
    ppermute x1, waiting for transfers between devices, extended(): lax.ppermute(lax.slice_in_dim(block, 0, width, axis=dim), axis, backward)  5.34 us
    dot_general x1, matrix products, on_device(): jnp.dot(normed, full_weights, preferred_element_type=jnp.float32)  4.87 us
  transfers between devices with their start and end apart: 5, of which 4 were waited for; matrix products, arithmetic and copies ran while one was open for 7% of the time, Pallas kernels for 0%

commit v1 on v0

v1 whole, which is shorter than its diff:
```python
import functools

import jax
import jax.numpy as jnp
from jax import lax
from jax.experimental import pallas as pl
from jax.experimental.pallas import tpu as pltpu
from jax.sharding import PartitionSpec as P

MESH = pl.DeviceIdType.MESH
D = 1024
ROWS = 256
SHARD = 96
SUB = 32
TAPS = 31
HALF = 15
NB = D // 128
LOG2E = 1.4426950408889634

ARRIVALS = (
    (-1, 0, "B"), (0, -1, "B"), (0, 1, "B"), (1, 0, "B"), (-1, 0, "A"), (0, -1, "A"), (0, 1, "A"), (1, 0, "A"),
    (2, 0, "B"), (-1, 0, "C"), (0, -1, "C"), (0, 1, "C"), (1, 0, "C"), (-1, 1, "B"), (1, 1, "B"), (0, 2, "B"),
    (2, 0, "A"), (2, 0, "C"), (-1, 1, "A"), (1, 1, "A"), (-1, -1, "B"), (1, -1, "B"), (-1, 1, "C"), (1, 1, "C"),
    (0, 2, "C"), (2, 1, "B"), (0, 2, "A"), (-1, 2, "B"), (-1, -1, "A"), (1, 2, "B"), (2, 1, "A"), (1, -1, "A"),
    (1, -1, "C"), (-1, -1, "C"), (2, -1, "B"), (2, 1, "C"), (2, 2, "B"), (2, -1, "A"), (-1, 2, "C"), (1, 2, "C"),
    (-1, 2, "A"), (1, 2, "A"), (2, -1, "C"), (2, 2, "C"), (2, 2, "A"),
)
RECV = {key: i for i, key in enumerate(ARRIVALS)}
RELAY = {"A": 1, "B": -1}
SHARDS = tuple((d1, d2) for d1 in (0, 1, -1, 2) for d2 in (0, 1, -1, 2))
PAIR = {}
for _d in SHARDS:
    if _d == (0, 0):
        PAIR[_d + ("own",)] = len(PAIR)
    else:
        PAIR[_d + ("AB",)] = len(PAIR)
        PAIR[_d + ("C",)] = len(PAIR)
ZSIGN = {}
for _key in ARRIVALS:
    if _key[2] == "B":
        ZSIGN[_key[:2]] = 1 if len(ZSIGN) % 2 == 0 else -1
NSEND = 160


def layer_norm(values):
    centred = values - jnp.mean(values, axis=-1, keepdims=True)
    return centred / jnp.sqrt(jnp.mean(centred * centred, axis=-1, keepdims=True) + 1e-05)


def kernel(
    x_hbm, w_hbm, wo_hbm, dw_ref, gain_ref, bias_ref, rec_ref, left_ref, out_ref,
    wbuf, xown, xprev, normed, qkv, wo, attended, bias_s, cbuf, cedge, halo, rcol, xs,
    loc_sem, send_sem, recv_sem, pair_sem, frame_sem, halo_sem,
):
    seq = lax.axis_index("seq")
    grp = lax.axis_index("grp")
    k = lax.rem(seq, 2)
    chip = seq // 2
    x, y = lax.rem(chip, 4), chip // 4
    i1 = x + k * (y - x)
    i2 = y + k * (x - y)
    st1 = 2 + 6 * k
    st2 = 8 - 6 * k
    par = lax.rem(grp, 2)
    other = 1 - k

    def seq_at(d1, d2):
        return lax.rem(i1 + d1 + 4, 4) * st1 + lax.rem(i2 + d2 + 4, 4) * st2 + k

    def pair_at(d1, d2):
        return lax.rem(i2 + d1 + 4, 4) * st2 + lax.rem(i1 + d2 + 4, 4) * st1 + other

    start_of = {"A": SUB, "B": 2 * SUB * par, "C": 2 * SUB * (1 - par), "AB": SUB * par, "own": 0}
    size_of = {"A": SUB, "B": SUB, "C": SUB, "AB": 2 * SUB, "own": SHARD}

    def rows_of(owner, piece):
        return pl.ds(pl.multiple_of(owner * SHARD + start_of[piece], SUB), size_of[piece])

    nxt, prv = lax.rem(seq + 1, 32), lax.rem(seq + 31, 32)
    partner = seq + 1 - 2 * k
    far = lax.rem(seq + 31 + 2 * k, 32)
    ax1 = {1: seq_at(1, 0), -1: seq_at(-1, 0)}
    ax2 = {1: seq_at(0, 1), -1: seq_at(0, -1)}
    zto = {1: lax.rem(grp + 1 + 14 * k, 16), -1: lax.rem(grp + 15 - 14 * k, 16)}
    sends = []

    local = [
        pltpu.make_async_copy(x_hbm, xown, loc_sem.at[0]),
        pltpu.make_async_copy(wo_hbm, wo, loc_sem.at[1]),
        pltpu.make_async_copy(
            w_hbm, wbuf.at[pl.ds(pl.multiple_of(seq * SHARD, SUB), SHARD)], loc_sem.at[2]
        ),
    ]
    for copy in local:
        copy.start()

    barrier = pltpu.get_barrier_semaphore()
    for target in (ax1[1], ax1[-1], ax2[1], ax2[-1], partner, far):
        pl.semaphore_signal(barrier, inc=1, device_id={"seq": target}, device_id_type=MESH)
    for sign in (1, -1):
        pl.semaphore_signal(barrier, inc=1, device_id={"grp": zto[sign]}, device_id_type=MESH)
    pl.semaphore_wait(barrier, 8)

    def send(src, dst, sem, where):
        copy = pltpu.make_async_remote_copy(
            src_ref=src, dst_ref=dst, send_sem=send_sem.at[len(sends)], recv_sem=sem, device_id=where,
            device_id_type=MESH,
        )
        copy.start()
        sends.append(copy)

    def forward(rel, piece, where, key):
        rows = rows_of(seq_at(*rel), piece)
        send(wbuf.at[rows], wbuf.at[rows], recv_sem.at[RECV[key]], where)

    def to_pair(rel, piece):
        rows = rows_of(seq_at(*rel), piece)
        send(wbuf.at[rows], wbuf.at[rows], pair_sem.at[PAIR[rel + (piece,)]], {"seq": partner})

    for piece in ("B", "A"):
        source = w_hbm.at[pl.ds(pl.multiple_of(start_of[piece] + 0 * seq, SUB), SUB)]
        target = wbuf.at[rows_of(seq, piece)]
        for sign in (1, -1):
            send(source, target, recv_sem.at[RECV[-sign, 0, piece]], {"seq": ax1[sign]})
        for sign in (1, -1):
            send(source, target, recv_sem.at[RECV[0, -sign, piece]], {"seq": ax2[sign]})
    own_rows = pl.ds(pl.multiple_of(seq * SHARD, SUB), SHARD)
    send(w_hbm, wbuf.at[own_rows], pair_sem.at[PAIR[0, 0, "own"]], {"seq": partner})
    for part in range(4):
        rows = pl.ds(part * 64, 64)
        send(x_hbm.at[rows], xprev.at[rows], frame_sem.at[part], {"seq": nxt})

    local[0].wait()
    normed[ROWS:] = layer_norm(xown[...].astype(jnp.float32)).astype(jnp.bfloat16)
    first = 2 * seq
    spans = [
        rec_ref[pl.ds(lax.rem(first + o + 64, 64), 1), :] for o in (-2, -1, 0, 1, 2)
    ]
    missing = jnp.full((1, 128), -1, jnp.int32)
    spans[0] = jnp.where(seq > 0, spans[0], missing)
    spans[1] = jnp.where(seq > 0, spans[1], missing)
    spans[4] = jnp.where(seq < 31, spans[4], missing)
    cols = [jnp.transpose(jnp.broadcast_to(row, (128, 128))) for row in spans]
    rcol[0:16] = cols[1][112:128]
    rcol[16:144] = cols[2]
    rcol[144:272] = cols[3]
    rcol[272:288] = cols[4][0:16]
    for span in range(2):
        left = left_ref[first + span]
        for block in range(3):
            keys = spans[span + block]
            if block < 2:
                keys = jnp.where(left >= 2 - block, keys, missing)
            same = jnp.broadcast_to(keys, (128, 128)) == cols[span + 2]
            bias_s[span, :, block * 128 : block * 128 + 128] = jnp.where(same, 0.0, -1e30)

    arrived = set()
    for key in ARRIVALS:
        d1, d2, piece = key
        rel = (d1, d2)
        rows = rows_of(seq_at(d1, d2), piece)
        pltpu.make_async_copy(wbuf.at[rows], wbuf.at[rows], recv_sem.at[RECV[key]]).wait()
        arrived.add(key)
        if piece == "C":
            to_pair(rel, "C")
            continue
        if d2 == 0:
            if d1 == -RELAY[piece]:
                forward(rel, piece, {"seq": ax1[RELAY[piece]]}, (2, 0, piece))
            for sign in (1, -1):
                forward(rel, piece, {"seq": ax2[sign]}, (d1, -sign, piece))
        elif d2 == -RELAY[piece]:
            forward(rel, piece, {"seq": ax2[RELAY[piece]]}, (d1, 2, piece))
        if piece == "B":
            forward(rel, piece, {"grp": zto[ZSIGN[rel]]}, rel + ("C",))
        if rel + ("A",) in arrived and rel + ("B",) in arrived:
            to_pair(rel, "AB")

    for part in range(4):
        rows = pl.ds(part * 64, 64)
        pltpu.make_async_copy(xprev.at[rows], xprev.at[rows], frame_sem.at[part]).wait()
    normed[:ROWS] = layer_norm(xprev[...].astype(jnp.float32)).astype(jnp.bfloat16)
    for d1, d2, piece in PAIR:
        rows = rows_of(pair_at(d1, d2), piece)
        pltpu.make_async_copy(wbuf.at[rows], wbuf.at[rows], pair_sem.at[PAIR[d1, d2, piece]]).wait()
    local[2].wait()

    @pl.loop(0, 12)
    def _(block):
        rows = pl.ds(pl.multiple_of(block * 256, 256), 256)
        part = lax.dot_general(
            normed[...], wbuf[rows, :], (((1,), (1,)), ((), ())), preferred_element_type=jnp.float32
        ).astype(jnp.bfloat16)
        qkv[2 * block] = part[:, :128]
        qkv[2 * block + 1] = part[:, 128:]

    lane = lax.broadcasted_iota(jnp.int32, (128, 128), 1)
    low = lane < 64

    @pl.loop(0, NB)
    def _(pair):
        for span in range(2):
            q = qkv[pair, ROWS + span * 128 : ROWS + span * 128 + 128, :]
            keys = qkv[NB + pair, span * 128 : span * 128 + 384, :]
            values = qkv[2 * NB + pair, span * 128 : span * 128 + 384, :]
            zero = jnp.zeros_like(q)
            both = jnp.concatenate([jnp.where(low, q, zero), jnp.where(low, zero, q)], axis=0)
            scores = lax.dot_general(
                both, keys, (((1,), (1,)), ((), ())), preferred_element_type=jnp.float32
            )
            mask = bias_s[span]
            scores = scores * (0.125 * LOG2E) + jnp.concatenate([mask, mask], axis=0)
            expo = jnp.exp2(scores - jnp.max(scores, axis=-1, keepdims=True))
            total = jnp.sum(expo, axis=-1, keepdims=True)
            got = jnp.dot(expo.astype(jnp.bfloat16), values, preferred_element_type=jnp.float32)
            got = got / total
            attended[pair, span * 128 : span * 128 + 128, :] = jnp.where(
                low, got[:128], got[128:]
            ).astype(jnp.bfloat16)

    local[1].wait()
    flat = jnp.concatenate([attended[i] for i in range(NB)], axis=1)
    for part in range(4):
        lanes = slice(part * 256, part * 256 + 256)
        cbuf[:, lanes] = (
            xown[:, lanes].astype(jnp.float32)
            + jnp.dot(flat, wo[:, lanes], preferred_element_type=jnp.float32)
        ).astype(jnp.bfloat16)
    cnormed = layer_norm(cbuf[...].astype(jnp.float32)).astype(jnp.bfloat16)
    cedge[0] = cnormed[:16]
    cedge[1] = cnormed[ROWS - 16 :]
    send(cedge.at[0], halo.at[1], halo_sem.at[1], {"seq": prv})
    send(cedge.at[1], halo.at[0], halo_sem.at[0], {"seq": nxt})
    wide = cnormed.astype(jnp.float32)
    for i in range(NB):
        xs[i, 16 : 16 + ROWS, :] = wide[:, i * 128 : i * 128 + 128]
    for side in range(2):
        pltpu.make_async_copy(halo.at[side], halo.at[side], halo_sem.at[side]).wait()
        wide_halo = halo[side].astype(jnp.float32)
        for i in range(NB):
            xs[i, side * (ROWS + 16) : side * (ROWS + 16) + 16, :] = wide_halo[:, i * 128 : i * 128 + 128]

    tile = 16

    @pl.loop(0, ROWS // tile)
    def _(step):
        base = pl.multiple_of(step * tile, tile)
        own = rcol[pl.ds(base + 16, tile), :]
        sums = [jnp.zeros((tile, 128), jnp.float32) for _ in range(NB)]
        for tap in range(TAPS):
            same = rcol[pl.ds(base + tap + 1, tile), :] == own
            for i in range(NB):
                term = dw_ref[tap : tap + 1, i * 128 : i * 128 + 128] * xs[i, pl.ds(base + tap + 1, tile), :]
                sums[i] = sums[i] + jnp.where(same, term, 0.0)
        for i in range(NB):
            lanes = slice(i * 128, i * 128 + 128)
            z = gain_ref[:, lanes] * sums[i] + bias_ref[:, lanes]
            mid = cbuf[pl.ds(base, tile), lanes].astype(jnp.float32)
            out_ref[pl.ds(base, tile), lanes] = (mid + z * jax.nn.sigmoid(z)).astype(jnp.bfloat16)

    for copy in sends:
        copy.wait_send()


def on_device(frames, w_qkv, w_out, dw_kernel, conv_gain, conv_bias, rec_ids, left_spans):
    vmem = pl.BlockSpec(memory_space=pltpu.VMEM)
    anyspace = pl.BlockSpec(memory_space=pl.ANY)
    bf = jnp.bfloat16
    return pl.pallas_call(
        kernel,
        out_shape=jax.ShapeDtypeStruct((ROWS, D), bf),
        in_specs=[anyspace, anyspace, anyspace, vmem, vmem, vmem, vmem,
                  pl.BlockSpec(memory_space=pltpu.SMEM)],
        out_specs=vmem,
        scratch_shapes=[
            pltpu.VMEM((3 * D, D), bf),
            pltpu.VMEM((ROWS, D), bf),
            pltpu.VMEM((ROWS, D), bf),
            pltpu.VMEM((2 * ROWS, D), bf),
            pltpu.VMEM((3 * NB, 2 * ROWS, 128), bf),
            pltpu.VMEM((D, D), bf),
            pltpu.VMEM((NB, ROWS, 128), bf),
            pltpu.VMEM((2, 128, 384), jnp.float32),
            pltpu.VMEM((ROWS, D), bf),
            pltpu.VMEM((2, 16, D), bf),
            pltpu.VMEM((2, 16, D), bf),
            pltpu.VMEM((ROWS + 32, 128), jnp.int32),
            pltpu.VMEM((NB, ROWS + 32, 128), jnp.float32),
            pltpu.SemaphoreType.DMA((3,)),
            pltpu.SemaphoreType.DMA((NSEND,)),
            pltpu.SemaphoreType.DMA((len(ARRIVALS),)),
            pltpu.SemaphoreType.DMA((len(PAIR),)),
            pltpu.SemaphoreType.DMA((4,)),
            pltpu.SemaphoreType.DMA((2,)),
        ],
        compiler_params=pltpu.CompilerParams(
            collective_id=0, has_side_effects=True, vmem_limit_bytes=56 * 1024 * 1024
        ),
    )(
        frames, jnp.transpose(w_qkv), w_out, dw_kernel, conv_gain.reshape(1, D), conv_bias.reshape(1, D),
        rec_ids.reshape(64, 128), left_spans,
    )


def solution(mesh):
    in_specs = (P(("grp", "seq"), None), P(None, "seq"), P(), P(), P(), P(), P("grp"), P("grp"))
    out_specs = P(("grp", "seq"), None)
    return jax.shard_map(
        on_device, mesh=mesh, in_specs=in_specs, out_specs=out_specs, check_vma=False
    )
```

time: 169 us -> 63.4 us (0.38)
  the two profiles are of different devices: /device:TPU:7 before, /device:TPU:1 now
where the time goes in v1:
time: 63.4 us; the launch traced here: 62.9 us
  Pallas kernels  61.1 us (96%)
  local copies, waits for them, and re-layouts  1.87 us (3%)
    pallas_call x1, Pallas kernels, on_device(): pl.pallas_call(kernel, out_shape=jax.ShapeDtypeStruct((ROWS, D), bf), in_...  61.1 us
    unnamed x1, local copies, waits for them, and re-layouts  1.87 us

profile of v1, /device:TPU:1, one launch (start us, length us, event | category | flops | bytes accessed | tf_op | source)
XLA Modules:
  0.0 62.9 jit_solution(18125069104589308836)
XLA Ops:
  0.0 61.1 %shard_map.82 = bf16[256,1024]{1,0:T(8,128)(2,1)} custom-call(bf16[256,1024]{1,0:T(8,128)(2,1)} %x_hbm.1, bf16[96,1024]{1,0:T(8,128)(2,1)} %bitcast.4, bf16[1024,1024]{1,0:T(8,128)(2,1)} %wo_hbm.1, f32[31,1024]{1,0:T(8,128)} %dw_ref.1, f32[1,1024]{1,0:T(1,128)} %bitcast.6, f32[1,1024]{1,0:T(1,128)} %bitcast.7, s32[64,128]{1,0:T(8,128)} %bitcast.5, s32[64]{0:T(128)} %left_ref.1), custom_call_target="tpu_custom_call" | custom-call | tf_op jit(solution)/shard_map/pallas_call | solution.py:269
  61.1 1.9 %copy.10 = bf16[256,1024]{1,0:T(8,128)(2,1)} copy(bf16[256,1024]{1,0:T(8,128)(2,1)} %shard_map.82) | data formatting | bytes 1048576

commit v2 on v1

--- a/solution.py
+++ b/solution.py
@@ -11,35 +11,31 @@
 D = 1024
 ROWS = 256
 SHARD = 96
-SUB = 32
 TAPS = 31
 HALF = 15
 NB = D // 128
 LOG2E = 1.4426950408889634
 
 ARRIVALS = (
-    (-1, 0, "B"), (0, -1, "B"), (0, 1, "B"), (1, 0, "B"), (-1, 0, "A"), (0, -1, "A"), (0, 1, "A"), (1, 0, "A"),
-    (2, 0, "B"), (-1, 0, "C"), (0, -1, "C"), (0, 1, "C"), (1, 0, "C"), (-1, 1, "B"), (1, 1, "B"), (0, 2, "B"),
-    (2, 0, "A"), (2, 0, "C"), (-1, 1, "A"), (1, 1, "A"), (-1, -1, "B"), (1, -1, "B"), (-1, 1, "C"), (1, 1, "C"),
-    (0, 2, "C"), (2, 1, "B"), (0, 2, "A"), (-1, 2, "B"), (-1, -1, "A"), (1, 2, "B"), (2, 1, "A"), (1, -1, "A"),
-    (1, -1, "C"), (-1, -1, "C"), (2, -1, "B"), (2, 1, "C"), (2, 2, "B"), (2, -1, "A"), (-1, 2, "C"), (1, 2, "C"),
-    (-1, 2, "A"), (1, 2, "A"), (2, -1, "C"), (2, 2, "C"), (2, 2, "A"),
+    (1, 0, "A"), (-1, 0, "A"), (1, 0, "C"), (-1, 0, "C"), (1, 0, "B"), (0, 1, "A"), (-1, 0, "B"), (2, 0, "A"),
+    (0, -1, "A"), (0, 1, "C"), (1, -1, "A"), (0, -1, "C"), (2, 0, "C"), (-1, -1, "A"), (0, -1, "B"), (1, 1, "A"),
+    (0, 1, "B"), (-1, 1, "A"), (2, 0, "B"), (1, -1, "C"), (1, 1, "C"), (-1, -1, "C"), (-1, 1, "C"), (2, 1, "A"),
+    (0, 2, "C"), (1, 1, "B"), (2, 1, "C"), (-1, 1, "B"), (1, -1, "B"), (0, 2, "B"), (2, -1, "A"), (1, 2, "C"),
+    (-1, -1, "B"), (0, 2, "A"), (1, 2, "A"), (2, -1, "C"), (2, 1, "B"), (-1, 2, "C"), (-1, 2, "A"), (1, 2, "B"),
+    (-1, 2, "B"), (2, -1, "B"), (2, 2, "A"), (2, 2, "C"), (2, 2, "B"),
 )
 RECV = {key: i for i, key in enumerate(ARRIVALS)}
+START = {"A": 0, "C": 16, "B": 48, "AC": 0, "own": 0}
+SIZE = {"A": 16, "C": 32, "B": 48, "AC": 48, "own": SHARD}
 RELAY = {"A": 1, "B": -1}
 SHARDS = tuple((d1, d2) for d1 in (0, 1, -1, 2) for d2 in (0, 1, -1, 2))
 PAIR = {}
 for _d in SHARDS:
-    if _d == (0, 0):
-        PAIR[_d + ("own",)] = len(PAIR)
-    else:
-        PAIR[_d + ("AB",)] = len(PAIR)
-        PAIR[_d + ("C",)] = len(PAIR)
-ZSIGN = {}
-for _key in ARRIVALS:
-    if _key[2] == "B":
-        ZSIGN[_key[:2]] = 1 if len(ZSIGN) % 2 == 0 else -1
-NSEND = 160
+    for _piece in ("own",) if _d == (0, 0) else ("AC", "B"):
+        PAIR[_d + (_piece,)] = len(PAIR)
+FRAME_PARTS = {0: 0, 6: 1, 12: 2, 18: 3}
+GROUPS = {37: 0, 42: 1, 43: -1}
+NSEND = 128
 
 
 def layer_norm(values):
@@ -53,7 +49,6 @@
     loc_sem, send_sem, recv_sem, pair_sem, frame_sem, halo_sem,
 ):
     seq = lax.axis_index("seq")
-    grp = lax.axis_index("grp")
     k = lax.rem(seq, 2)
     chip = seq // 2
     x, y = lax.rem(chip, 4), chip // 4
@@ -61,8 +56,9 @@
     i2 = y + k * (x - y)
     st1 = 2 + 6 * k
     st2 = 8 - 6 * k
-    par = lax.rem(grp, 2)
     other = 1 - k
+    turn1 = 2 * k - 1
+    turn2 = 1 - 2 * k
 
     def seq_at(d1, d2):
         return lax.rem(i1 + d1 + 4, 4) * st1 + lax.rem(i2 + d2 + 4, 4) * st2 + k
@@ -70,25 +66,21 @@
     def pair_at(d1, d2):
         return lax.rem(i2 + d1 + 4, 4) * st2 + lax.rem(i1 + d2 + 4, 4) * st1 + other
 
-    start_of = {"A": SUB, "B": 2 * SUB * par, "C": 2 * SUB * (1 - par), "AB": SUB * par, "own": 0}
-    size_of = {"A": SUB, "B": SUB, "C": SUB, "AB": 2 * SUB, "own": SHARD}
-
     def rows_of(owner, piece):
-        return pl.ds(pl.multiple_of(owner * SHARD + start_of[piece], SUB), size_of[piece])
+        return pl.ds(pl.multiple_of(owner * SHARD + START[piece], 16), SIZE[piece])
 
     nxt, prv = lax.rem(seq + 1, 32), lax.rem(seq + 31, 32)
     partner = seq + 1 - 2 * k
     far = lax.rem(seq + 31 + 2 * k, 32)
     ax1 = {1: seq_at(1, 0), -1: seq_at(-1, 0)}
     ax2 = {1: seq_at(0, 1), -1: seq_at(0, -1)}
-    zto = {1: lax.rem(grp + 1 + 14 * k, 16), -1: lax.rem(grp + 15 - 14 * k, 16)}
     sends = []
 
     local = [
         pltpu.make_async_copy(x_hbm, xown, loc_sem.at[0]),
         pltpu.make_async_copy(wo_hbm, wo, loc_sem.at[1]),
         pltpu.make_async_copy(
-            w_hbm, wbuf.at[pl.ds(pl.multiple_of(seq * SHARD, SUB), SHARD)], loc_sem.at[2]
+            w_hbm, wbuf.at[pl.ds(pl.multiple_of(seq * SHARD, 16), SHARD)], loc_sem.at[2]
         ),
     ]
     for copy in local:
@@ -97,9 +89,7 @@
     barrier = pltpu.get_barrier_semaphore()
     for target in (ax1[1], ax1[-1], ax2[1], ax2[-1], partner, far):
         pl.semaphore_signal(barrier, inc=1, device_id={"seq": target}, device_id_type=MESH)
-    for sign in (1, -1):
-        pl.semaphore_signal(barrier, inc=1, device_id={"grp": zto[sign]}, device_id_type=MESH)
-    pl.semaphore_wait(barrier, 8)
+    pl.semaphore_wait(barrier, 6)
 
     def send(src, dst, sem, where):
         copy = pltpu.make_async_remote_copy(
@@ -109,26 +99,28 @@
         copy.start()
         sends.append(copy)
 
-    def forward(rel, piece, where, key):
-        rows = rows_of(seq_at(*rel), piece)
-        send(wbuf.at[rows], wbuf.at[rows], recv_sem.at[RECV[key]], where)
+    def forward(owner, piece, where, key):
+        rows = rows_of(owner, piece)
+        send(wbuf.at[rows], wbuf.at[rows], recv_sem.at[RECV[key]], {"seq": where})
 
     def to_pair(rel, piece):
         rows = rows_of(seq_at(*rel), piece)
         send(wbuf.at[rows], wbuf.at[rows], pair_sem.at[PAIR[rel + (piece,)]], {"seq": partner})
 
-    for piece in ("B", "A"):
-        source = w_hbm.at[pl.ds(pl.multiple_of(start_of[piece] + 0 * seq, SUB), SUB)]
+    def send_frames(part):
+        rows = pl.ds(part * 64, 64)
+        send(x_hbm.at[rows], xprev.at[rows], frame_sem.at[part], {"seq": nxt})
+
+    for piece in ("A", "C", "B"):
+        source = w_hbm.at[pl.ds(START[piece], SIZE[piece])]
         target = wbuf.at[rows_of(seq, piece)]
         for sign in (1, -1):
             send(source, target, recv_sem.at[RECV[-sign, 0, piece]], {"seq": ax1[sign]})
         for sign in (1, -1):
             send(source, target, recv_sem.at[RECV[0, -sign, piece]], {"seq": ax2[sign]})
-    own_rows = pl.ds(pl.multiple_of(seq * SHARD, SUB), SHARD)
+    own_rows = pl.ds(pl.multiple_of(seq * SHARD, 16), SHARD)
     send(w_hbm, wbuf.at[own_rows], pair_sem.at[PAIR[0, 0, "own"]], {"seq": partner})
-    for part in range(4):
-        rows = pl.ds(part * 64, 64)
-        send(x_hbm.at[rows], xprev.at[rows], frame_sem.at[part], {"seq": nxt})
+    send_frames(FRAME_PARTS[0])
 
     local[0].wait()
     normed[ROWS:] = layer_norm(xown[...].astype(jnp.float32)).astype(jnp.bfloat16)
@@ -154,45 +146,76 @@
             same = jnp.broadcast_to(keys, (128, 128)) == cols[span + 2]
             bias_s[span, :, block * 128 : block * 128 + 128] = jnp.where(same, 0.0, -1e30)
 
+    taken = set()
+
+    def from_pair(shards):
+        for key in PAIR:
+            if key[:2] in shards and key not in taken:
+                taken.add(key)
+                rows = rows_of(pair_at(key[0], key[1]), key[2])
+                pltpu.make_async_copy(wbuf.at[rows], wbuf.at[rows], pair_sem.at[PAIR[key]]).wait()
+
+    def project(dy):
+        from_pair([d for d in SHARDS if dy in d])
+        first_block = 3 * lax.rem(y + dy + 4, 4)
+
+        @pl.loop(0, 3)
+        def _(j):
+            block = first_block + j
+            rows = pl.ds(pl.multiple_of(block * 256, 256), 256)
+
+            @pl.when(block < 4)
+            def _():
+                part = lax.dot_general(
+                    normed[ROWS:, :], wbuf[rows, :], (((1,), (1,)), ((), ())), preferred_element_type=jnp.float32
+                ).astype(jnp.bfloat16)
+                qkv[2 * block, ROWS:, :] = part[:, :128]
+                qkv[2 * block + 1, ROWS:, :] = part[:, 128:]
+
+            @pl.when(block >= 4)
+            def _():
+                part = lax.dot_general(
+                    normed[...], wbuf[rows, :], (((1,), (1,)), ((), ())), preferred_element_type=jnp.float32
+                ).astype(jnp.bfloat16)
+                qkv[2 * block] = part[:, :128]
+                qkv[2 * block + 1] = part[:, 128:]
+
     arrived = set()
-    for key in ARRIVALS:
+    for count, key in enumerate(ARRIVALS, 1):
         d1, d2, piece = key
         rel = (d1, d2)
-        rows = rows_of(seq_at(d1, d2), piece)
+        owner = seq_at(d1, d2)
+        rows = rows_of(owner, piece)
         pltpu.make_async_copy(wbuf.at[rows], wbuf.at[rows], recv_sem.at[RECV[key]]).wait()
         arrived.add(key)
-        if piece == "C":
-            to_pair(rel, "C")
-            continue
         if d2 == 0:
-            if d1 == -RELAY[piece]:
-                forward(rel, piece, {"seq": ax1[RELAY[piece]]}, (2, 0, piece))
+            if piece == "C":
+                if {(1, 0, "C"), (-1, 0, "C")} <= arrived and d1 != 2:
+                    forward(seq_at(-turn1, 0), "C", seq_at(turn1, 0), (2, 0, "C"))
+            elif d1 == -RELAY[piece]:
+                forward(owner, piece, ax1[RELAY[piece]], (2, 0, piece))
             for sign in (1, -1):
-                forward(rel, piece, {"seq": ax2[sign]}, (d1, -sign, piece))
+                forward(owner, piece, ax2[sign], (d1, -sign, piece))
+        elif piece == "C":
+            if {(d1, 1, "C"), (d1, -1, "C")} <= arrived and d2 != 2:
+                forward(seq_at(d1, -turn2), "C", seq_at(0, turn2), (d1, 2, "C"))
         elif d2 == -RELAY[piece]:
-            forward(rel, piece, {"seq": ax2[RELAY[piece]]}, (d1, 2, piece))
+            forward(owner, piece, ax2[RELAY[piece]], (d1, 2, piece))
         if piece == "B":
-            forward(rel, piece, {"grp": zto[ZSIGN[rel]]}, rel + ("C",))
-        if rel + ("A",) in arrived and rel + ("B",) in arrived:
-            to_pair(rel, "AB")
-
-    for part in range(4):
-        rows = pl.ds(part * 64, 64)
-        pltpu.make_async_copy(xprev.at[rows], xprev.at[rows], frame_sem.at[part]).wait()
-    normed[:ROWS] = layer_norm(xprev[...].astype(jnp.float32)).astype(jnp.bfloat16)
-    for d1, d2, piece in PAIR:
-        rows = rows_of(pair_at(d1, d2), piece)
-        pltpu.make_async_copy(wbuf.at[rows], wbuf.at[rows], pair_sem.at[PAIR[d1, d2, piece]]).wait()
-    local[2].wait()
-
-    @pl.loop(0, 12)
-    def _(block):
-        rows = pl.ds(pl.multiple_of(block * 256, 256), 256)
-        part = lax.dot_general(
-            normed[...], wbuf[rows, :], (((1,), (1,)), ((), ())), preferred_element_type=jnp.float32
-        ).astype(jnp.bfloat16)
-        qkv[2 * block] = part[:, :128]
-        qkv[2 * block + 1] = part[:, 128:]
+            to_pair(rel, "B")
+        elif rel + ("A",) in arrived and rel + ("C",) in arrived:
+            to_pair(rel, "AC")
+        if count in FRAME_PARTS:
+            send_frames(FRAME_PARTS[count])
+        if count == 33:
+            for part in range(4):
+                rows = pl.ds(part * 64, 64)
+                pltpu.make_async_copy(xprev.at[rows], xprev.at[rows], frame_sem.at[part]).wait()
+            normed[:ROWS] = layer_norm(xprev[...].astype(jnp.float32)).astype(jnp.bfloat16)
+            local[2].wait()
+        if count in GROUPS:
+            project(GROUPS[count])
+    project(2)
 
     lane = lax.broadcasted_iota(jnp.int32, (128, 128), 1)
     low = lane < 64
@@ -234,17 +257,9 @@
     wide = cnormed.astype(jnp.float32)
     for i in range(NB):
         xs[i, 16 : 16 + ROWS, :] = wide[:, i * 128 : i * 128 + 128]
-    for side in range(2):
-        pltpu.make_async_copy(halo.at[side], halo.at[side], halo_sem.at[side]).wait()
-        wide_halo = halo[side].astype(jnp.float32)
-        for i in range(NB):
-            xs[i, side * (ROWS + 16) : side * (ROWS + 16) + 16, :] = wide_halo[:, i * 128 : i * 128 + 128]
-
     tile = 16
 
-    @pl.loop(0, ROWS // tile)
-    def _(step):
-        base = pl.multiple_of(step * tile, tile)
+    def convolve(base):
         own = rcol[pl.ds(base + 16, tile), :]
         sums = [jnp.zeros((tile, 128), jnp.float32) for _ in range(NB)]
         for tap in range(TAPS):
@@ -257,6 +272,20 @@
             z = gain_ref[:, lanes] * sums[i] + bias_ref[:, lanes]
             mid = cbuf[pl.ds(base, tile), lanes].astype(jnp.float32)
             out_ref[pl.ds(base, tile), lanes] = (mid + z * jax.nn.sigmoid(z)).astype(jnp.bfloat16)
+
+    @pl.loop(1, ROWS // tile - 1)
+    def _(step):
+        convolve(pl.multiple_of(step * tile, tile))
+
+    for side in range(2):
+        pltpu.make_async_copy(halo.at[side], halo.at[side], halo_sem.at[side]).wait()
+        wide_halo = halo[side].astype(jnp.float32)
+        for i in range(NB):
+            xs[i, side * (ROWS + 16) : side * (ROWS + 16) + 16, :] = wide_halo[:, i * 128 : i * 128 + 128]
+
+    @pl.loop(0, 2)
+    def _(step):
+        convolve(pl.multiple_of(step * (ROWS - tile), tile))
 
     for copy in sends:
         copy.wait_send()

time: 63.4 us -> 57.3 us (0.904)
  Pallas kernels: 61.1 us -> 55.2 us
    pallas_call x1, Pallas kernels: 61.1 us -> 55.2 us  [on_device(): pl.pallas_call(kernel, out_shape=jax.ShapeDtypeStruct((ROWS, D), bf), in_...]
where the time goes in v2:
time: 57.3 us; the launch traced here: 57.1 us
  Pallas kernels  55.2 us (96%)
  local copies, waits for them, and re-layouts  1.87 us (3%)
    pallas_call x1, Pallas kernels, on_device(): pl.pallas_call(kernel, out_shape=jax.ShapeDtypeStruct((ROWS, D), bf), in_...  55.2 us
    unnamed x1, local copies, waits for them, and re-layouts  1.87 us

profile of v2, /device:TPU:1, one launch (start us, length us, event | category | flops | bytes accessed | tf_op | source)
XLA Modules:
  0.0 57.1 jit_solution(15005239749966220455)
XLA Ops:
  0.0 55.2 %shard_map.82 = bf16[256,1024]{1,0:T(8,128)(2,1)} custom-call(bf16[256,1024]{1,0:T(8,128)(2,1)} %x_hbm.1, bf16[96,1024]{1,0:T(8,128)(2,1)} %bitcast.4, bf16[1024,1024]{1,0:T(8,128)(2,1)} %wo_hbm.1, f32[31,1024]{1,0:T(8,128)} %dw_ref.1, f32[1,1024]{1,0:T(1,128)} %bitcast.6, f32[1,1024]{1,0:T(1,128)} %bitcast.7, s32[64,128]{1,0:T(8,128)} %bitcast.5, s32[64]{0:T(128)} %left_ref.1), custom_call_target="tpu_custom_call" | custom-call | tf_op jit(solution)/shard_map/pallas_call | solution.py:298
  55.3 1.9 %copy.10 = bf16[256,1024]{1,0:T(8,128)(2,1)} copy(bf16[256,1024]{1,0:T(8,128)(2,1)} %shard_map.82) | data formatting | bytes 1048576

commit v3 on v2

--- a/solution.py
+++ b/solution.py
@@ -220,8 +220,7 @@
     lane = lax.broadcasted_iota(jnp.int32, (128, 128), 1)
     low = lane < 64
 
-    @pl.loop(0, NB)
-    def _(pair):
+    def attend(pair, _):
         for span in range(2):
             q = qkv[pair, ROWS + span * 128 : ROWS + span * 128 + 128, :]
             keys = qkv[NB + pair, span * 128 : span * 128 + 384, :]
@@ -240,6 +239,9 @@
             attended[pair, span * 128 : span * 128 + 128, :] = jnp.where(
                 low, got[:128], got[128:]
             ).astype(jnp.bfloat16)
+        return 0
+
+    lax.fori_loop(0, NB, attend, 0, unroll=4)
 
     local[1].wait()
     flat = jnp.concatenate([attended[i] for i in range(NB)], axis=1)
@@ -257,9 +259,7 @@
     wide = cnormed.astype(jnp.float32)
     for i in range(NB):
         xs[i, 16 : 16 + ROWS, :] = wide[:, i * 128 : i * 128 + 128]
-    tile = 16
-
-    def convolve(base):
+    def convolve(base, tile):
         own = rcol[pl.ds(base + 16, tile), :]
         sums = [jnp.zeros((tile, 128), jnp.float32) for _ in range(NB)]
         for tap in range(TAPS):
@@ -273,9 +273,9 @@
             mid = cbuf[pl.ds(base, tile), lanes].astype(jnp.float32)
             out_ref[pl.ds(base, tile), lanes] = (mid + z * jax.nn.sigmoid(z)).astype(jnp.bfloat16)
 
-    @pl.loop(1, ROWS // tile - 1)
+    @pl.loop(0, 7)
     def _(step):
-        convolve(pl.multiple_of(step * tile, tile))
+        convolve(pl.multiple_of(step * 32 + 16, 16), 32)
 
     for side in range(2):
         pltpu.make_async_copy(halo.at[side], halo.at[side], halo_sem.at[side]).wait()
@@ -285,7 +285,7 @@
 
     @pl.loop(0, 2)
     def _(step):
-        convolve(pl.multiple_of(step * (ROWS - tile), tile))
+        convolve(pl.multiple_of(step * (ROWS - 16), 16), 16)
 
     for copy in sends:
         copy.wait_send()
@@ -297,7 +297,7 @@
     bf = jnp.bfloat16
     return pl.pallas_call(
         kernel,
-        out_shape=jax.ShapeDtypeStruct((ROWS, D), bf),
+        out_shape=pltpu.VMEM((ROWS, D), bf),
         in_specs=[anyspace, anyspace, anyspace, vmem, vmem, vmem, vmem,
                   pl.BlockSpec(memory_space=pltpu.SMEM)],
         out_specs=vmem,

time: 57.3 us -> 53.8 us (0.939)
  Pallas kernels: 55.2 us -> 52.8 us
  local copies, waits for them, and re-layouts: 1.87 us -> 0.8 us
    pallas_call x1, Pallas kernels: 55.2 us -> 52.8 us  [on_device(): pl.pallas_call(kernel, out_shape=pltpu.VMEM((ROWS, D), bf), in_specs=[any...]
    unnamed x1, local copies, waits for them, and re-layouts: 1.87 us -> 0.8 us
where the time goes in v3:
time: 53.8 us; the launch traced here: 53.6 us
  Pallas kernels  52.8 us (98%)
  local copies, waits for them, and re-layouts  0.8 us (1%)
    pallas_call x1, Pallas kernels, on_device(): pl.pallas_call(kernel, out_shape=pltpu.VMEM((ROWS, D), bf), in_specs=[any...  52.8 us

profile of v3, /device:TPU:1, one launch (start us, length us, event | category | flops | bytes accessed | tf_op | source)
XLA Modules:
  0.0 53.6 jit_solution(2175545576331863820)
XLA Ops:
  0.0 52.8 %shard_map.82 = bf16[256,1024]{1,0:T(8,128)(2,1)S(1)} custom-call(bf16[256,1024]{1,0:T(8,128)(2,1)} %x_hbm.1, bf16[96,1024]{1,0:T(8,128)(2,1)} %bitcast.4, bf16[1024,1024]{1,0:T(8,128)(2,1)} %wo_hbm.1, f32[31,1024]{1,0:T(8,128)} %dw_ref.1, f32[1,1024]{1,0:T(1,128)} %bitcast.6, f32[1,1024]{1,0:T(1,128)} %bitcast.7, s32[64,128]{1,0:T(8,128)} %bitcast.5, ...), custom_call_target="tpu_custom_call" | custom-call | tf_op jit(solution)/shard_map/pallas_call | solution.py:298
  52.8 0.8 %copy.10 = bf16[256,1024]{1,0:T(8,128)(2,1)} copy(bf16[256,1024]{1,0:T(8,128)(2,1)S(1)} %shard_map.82) | data formatting | bytes 1048576
